TPU v7x, 32 devices: a whole 2x2x4 slice. The times are simulated.
32 devices in a mesh: gx: 16 (over z, x, core), gy: 2 (over y).
Axes of the slice: x: 2, y: 2, z: 4, core: 2. Of those that a mesh axis runs over, the one named last changes fastest.
Arguments:
- fine_old: float32 [2, 3, 40, 32, 512], P(None, None, None, 'gx', 'gy'), may hold values from -6 to 6
- fine_now: float32 [2, 3, 40, 32, 512], P(None, None, None, 'gx', 'gy'), may hold values from -6 to 6
- coarse_old: float32 [2, 3, 80, 16, 256], P(None, None, None, 'gx', 'gy'), may hold values from -6 to 6
- coarse_now: float32 [2, 3, 80, 16, 256], P(None, None, None, 'gx', 'gy'), may hold values from -6 to 6
- shear_fine: float32 [40, 32, 512], P(None, 'gx', 'gy'), may hold values from 0.3 to 1.2
- lame_fine: float32 [40, 32, 512], P(None, 'gx', 'gy'), may hold values from 0.5 to 2
- shear_coarse: float32 [80, 16, 256], P(None, 'gx', 'gy'), may hold values from 0.3 to 1.2
- lame_coarse: float32 [80, 16, 256], P(None, 'gx', 'gy'), may hold values from 0.5 to 2
- topography: int32 [32, 512], P('gx', 'gy'), may hold values from 0 to 512
Outputs:
- fine_field: float32 [2, 3, 40, 32, 512], P(None, None, None, 'gx', 'gy')
- coarse_field: float32 [2, 3, 80, 16, 256], P(None, None, None, 'gx', 'gy')
- fine_kernel: float32 [40, 32, 512], P(None, 'gx', 'gy')
- coarse_kernel: float32 [80, 16, 256], P(None, 'gx', 'gy')
All inputs are finite; a program needn't handle non-finite values.
Results may differ from a plain program's by a relative error of at most 0.0003.
Values sent between devices are 32-bit elements; how exact they have to be, the bound alone decides.
A program may use at most 64 MiB of HBM per device.

v0:
```python
import jax
import jax.numpy as jnp
from jax import lax
from jax.sharding import PartitionSpec as P

STEPS = 2


STEP_SQUARED = 0.04


def with_halo(cells, sides, width):
    for axis, dim in sides:
        count = lax.axis_size(axis)
        ends = count - 1
        head = lax.slice_in_dim(cells, 0, width, axis=dim)
        tail = lax.slice_in_dim(cells, cells.shape[dim] - width, cells.shape[dim], axis=dim)
        cells = jnp.concatenate(
            [
                lax.ppermute(tail, axis, [(i, (i + 1) % count) for i in range(ends)]),
                cells,
                lax.ppermute(head, axis, [((i + 1) % count, i) for i in range(ends)]),
            ],
            axis=dim,
        )
    return cells


def offset(padded, up_down, along_x, along_y):
    depth_cells = padded.shape[2] - 2
    row_count = padded.shape[3] - 2
    column_count = padded.shape[4] - 2
    return padded[
        :,
        :,
        1 + up_down : 1 + up_down + depth_cells,
        1 + along_x : 1 + along_x + row_count,
        1 + along_y : 1 + along_y + column_count,
    ]


def accelerate(padded, spacing_pad, grid_step, shear, lame):
    center = offset(padded, 0, 0, 0)
    spacing = spacing_pad[1:-1, 1:-1]
    inverse_area = 1.0 / (grid_step * grid_step)
    curve_xx = (offset(padded, 0, 1, 0) - 2.0 * center + offset(padded, 0, -1, 0)) * inverse_area
    curve_yy = (offset(padded, 0, 0, 1) - 2.0 * center + offset(padded, 0, 0, -1)) * inverse_area
    curve_zz = (offset(padded, 1, 0, 0) - 2.0 * center + offset(padded, -1, 0, 0)) / (
        spacing * spacing
    )
    mixed_xy = (
        offset(padded, 0, 1, 1)
        - offset(padded, 0, 1, -1)
        - offset(padded, 0, -1, 1)
        + offset(padded, 0, -1, -1)
    ) * (0.25 * inverse_area)
    east_side = (offset(padded, 1, 1, 0) - offset(padded, -1, 1, 0)) / (2.0 * spacing_pad[2:, 1:-1])
    west_side = (offset(padded, 1, -1, 0) - offset(padded, -1, -1, 0)) / (
        2.0 * spacing_pad[:-2, 1:-1]
    )
    mixed_xz = (east_side - west_side) * (0.5 / grid_step)
    north_side = (offset(padded, 1, 0, 1) - offset(padded, -1, 0, 1)) / (
        2.0 * spacing_pad[1:-1, 2:]
    )
    south_side = (offset(padded, 1, 0, -1) - offset(padded, -1, 0, -1)) / (
        2.0 * spacing_pad[1:-1, :-2]
    )
    mixed_yz = (north_side - south_side) * (0.5 / grid_step)
    laplace = curve_xx + curve_yy + curve_zz
    grad_div = jnp.stack(
        [
            curve_xx[:, 0] + mixed_xy[:, 1] + mixed_xz[:, 2],
            mixed_xy[:, 0] + curve_yy[:, 1] + mixed_yz[:, 2],
            mixed_xz[:, 0] + mixed_yz[:, 1] + curve_zz[:, 2],
        ],
        axis=1,
    )
    return shear * laplace + (lame + shear) * grad_div


def restrict(plane):
    row_sums = plane[..., 0::2, :] + plane[..., 1::2, :]
    summed = row_sums[..., 0::2] + row_sums[..., 1::2]
    return 0.25 * summed


def prolong(padded_plane):
    middle = 0.75 * padded_plane[..., 1:-1, :]
    even_rows = middle + 0.25 * padded_plane[..., :-2, :]
    odd_rows = middle + 0.25 * padded_plane[..., 2:, :]
    plane_dims = even_rows.shape
    row_pairs = jnp.stack([even_rows, odd_rows], axis=-2).reshape(
        plane_dims[:-2] + (2 * plane_dims[-2], plane_dims[-1])
    )
    center_cols = 0.75 * row_pairs[..., 1:-1]
    even_cols = center_cols + 0.25 * row_pairs[..., :-2]
    odd_cols = center_cols + 0.25 * row_pairs[..., 2:]
    col_dims = even_cols.shape
    return jnp.stack([even_cols, odd_cols], axis=-1).reshape(col_dims[:-1] + (2 * col_dims[-1],))


def on_device(
    fine_old,
    fine_now,
    coarse_old,
    coarse_now,
    shear_fine,
    lame_fine,
    shear_coarse,
    lame_coarse,
    topography,
):
    heights = with_halo(topography, (("gx", 0), ("gy", 1)), 1)
    fine_space = 1.0 + heights.astype(jnp.float32) / 1024.0
    fine_kernel = jnp.zeros(shear_fine.shape, jnp.float32)
    coarse_kernel = jnp.zeros(shear_coarse.shape, jnp.float32)
    coarse_space = jnp.full((coarse_now.shape[3] + 2, coarse_now.shape[4] + 2), 2.0, jnp.float32)
    for time_level in range(STEPS):
        ridge = restrict(fine_now[:, :, -1])
        floor_plane = jnp.zeros_like(ridge)
        coarse_ext = jnp.concatenate(
            [ridge[:, :, None], coarse_now, floor_plane[:, :, None]], axis=2
        )
        coarse_pad = with_halo(coarse_ext, (("gx", 3), ("gy", 4)), 1)
        ghost = prolong(coarse_pad[:, :, 1])
        fine_ext = jnp.concatenate([fine_now[:, :, :1], fine_now, ghost[:, :, None]], axis=2)
        fine_pad = with_halo(fine_ext, (("gx", 3), ("gy", 4)), 1)
        fine_next = (
            2.0 * fine_now
            - fine_old
            + STEP_SQUARED * accelerate(fine_pad, fine_space, 1.0, shear_fine, lame_fine)
        )
        coarse_next = (
            2.0 * coarse_now
            - coarse_old
            + STEP_SQUARED * accelerate(coarse_pad, coarse_space, 2.0, shear_coarse, lame_coarse)
        )
        fine_kernel = fine_kernel + jnp.sum(fine_next[0] * fine_next[1], axis=0)
        coarse_kernel = coarse_kernel + jnp.sum(coarse_next[0] * coarse_next[1], axis=0)
        fine_old, fine_now = (fine_now, fine_next)
        coarse_old, coarse_now = (coarse_now, coarse_next)
    return (fine_now, coarse_now, fine_kernel, coarse_kernel)


def solution(mesh):
    return jax.shard_map(
        on_device,
        mesh=mesh,
        in_specs=(
            P(None, None, None, "gx", "gy"),
            P(None, None, None, "gx", "gy"),
            P(None, None, None, "gx", "gy"),
            P(None, None, None, "gx", "gy"),
            P(None, "gx", "gy"),
            P(None, "gx", "gy"),
            P(None, "gx", "gy"),
            P(None, "gx", "gy"),
            P("gx", "gy"),
        ),
        out_specs=(
            P(None, None, None, "gx", "gy"),
            P(None, None, None, "gx", "gy"),
            P(None, "gx", "gy"),
            P(None, "gx", "gy"),
        ),
        check_vma=False,
    )
```

profile of v0, /device:TPU:10, one launch (start us, length us, event | category | flops | bytes accessed | tf_op | source)
XLA Modules:
  0.0 151.6 jit_solution(1574733626199285986)
XLA Ops:
  0.7 1.5 copy.145
  2.6 1.1 copy.149
  3.9 1.9 %collective-permute-start.1 = (f32[2,3,82,1,128]{4,0,1,3,2:T(2,128)S(1)}, f32[2,3,82,1,128]{4,0,1,3,2:T(2,128)S(1)}, u32[]{:S(2)}, u32[]{:S(2)}) collective-permute-start(f32[2,3,82,1,128]{4,0,1,3,2:T(2,128)S(1)} %pad_maximum_fusion.19), channel_id=1, source_target_pairs={{2,0},{4,2},{6,4},{8,6},{10,8},{12,10},{14,12},{16,14},{18,16},{20... | collective-permute-start | bytes 755720 | tf_op jit(solution)/shard_map/ppermute | solution.py:22
  5.8 2.4 %collective-permute-start = (f32[2,3,82,1,128]{4,0,1,3,2:T(2,128)S(1)}, f32[2,3,82,1,128]{4,0,1,3,2:T(2,128)S(1)}, u32[]{:S(2)}, u32[]{:S(2)}) collective-permute-start(f32[2,3,82,1,128]{4,0,1,3,2:T(2,128)S(1)} %pad_maximum_fusion.19), channel_id=1, source_target_pairs={{0,2},{2,4},{4,6},{6,8},{8,10},{10,12},{12,14},{14,16},{16,18},{18... | collective-permute-start | bytes 755720 | tf_op jit(solution)/shard_map/ppermute | solution.py:20
  8.2 3.9 %collective-permute-start.8 = (s32[1,256]{1,0:T(1,128)S(1)}, s32[1,256]{1,0:T(1,128)S(1)}, u32[]{:S(2)}, u32[]{:S(2)}) collective-permute-start(s32[1,256]{1,0:T(1,128)S(1)} %get-tuple-element.98), channel_id=1, source_target_pairs={{0,2},{2,4},{4,6},{6,8},{8,10},{10,12},{12,14},{14,16},{16,18},{18... | collective-permute-start | bytes 3080 | tf_op jit(solution)/shard_map/ppermute | solution.py:20
  12.1 1.9 %collective-permute-start.9 = (s32[1,256]{1,0:T(1,128)S(1)}, s32[1,256]{1,0:T(1,128)S(1)}, u32[]{:S(2)}, u32[]{:S(2)}) collective-permute-start(s32[1,256]{1,0:T(1,128)S(1)} %get-tuple-element.99), channel_id=1, source_target_pairs={{2,0},{4,2},{6,4},{8,6},{10,8},{12,10},{14,12},{16,14},{18,16},{20... | collective-permute-start | bytes 3080 | tf_op jit(solution)/shard_map/ppermute | solution.py:22
  14.0 0.9 fusion.36
  15.4 3.4 %collective-permute-start.10 = (s32[4,1]{1,0:T(4,128)S(1)}, s32[4,1]{1,0:T(4,128)S(1)}, u32[]{:S(2)}, u32[]{:S(2)}) collective-permute-start(s32[4,1]{1,0:T(4,128)S(1)} %get-tuple-element.96), channel_id=1, source_target_pairs={{0,1},{2,3},{4,5},{6,7},{8,9},{10,11},{12,13},{14,15},{16,17},{18,... | collective-permute-start | bytes 56 | tf_op jit(solution)/shard_map/ppermute | solution.py:20
  18.8 1.3 collective-permute-start.11
  20.1 4.2 %collective-permute-done.11 = s32[4,1]{1,0:T(4,128)S(1)} collective-permute-done((s32[4,1]{1,0:T(4,128)S(1)}, s32[4,1]{1,0:T(4,128)S(1)}, u32[]{:S(2)}, u32[]{:S(2)}) %collective-permute-start.11) | collective-permute-done | bytes 48 | tf_op jit(solution)/shard_map/ppermute | solution.py:22
  24.7 1.0 fusion.102
  26.6 1.3 collective-permute-start.3
  27.9 4.5 %collective-permute-start.2 = (f32[2,3,82,3,1]{2,0,4,3,1:T(2,128)S(1)}, f32[2,3,82,3,1]{2,0,4,3,1:T(2,128)S(1)}, u32[]{:S(2)}, u32[]{:S(2)}) collective-permute-start(f32[2,3,82,3,1]{2,0,4,3,1:T(2,128)S(1)} %copy.150), channel_id=1, source_target_pairs={{0,1},{2,3},{4,5},{6,7},{8,9},{10,11},{12,13},{14,15},{16,17},{18,... | collective-permute-start | bytes 17720 | tf_op jit(solution)/shard_map/ppermute | solution.py:20
  32.5 1.3 collective-permute-done.2
  35.0 1.2 copy.184
  36.2 1.6 %reshape.216 = f32[2,3,1,2,256]{4,0,1,3,2:T(2,128)S(1)} reshape(f32[2,3,2,128,2]{4,3,0,1,2:T(8,128)} %copy.184) | data formatting | bytes 24576 | tf_op jit(solution)/shard_map/broadcast_in_dim;reshape | solution.py:126
  38.2 1.9 %collective-permute-start.5 = (f32[2,3,42,1,256]{4,0,1,3,2:T(2,128)S(1)}, f32[2,3,42,1,256]{4,0,1,3,2:T(2,128)S(1)}, u32[]{:S(2)}, u32[]{:S(2)}) collective-permute-start(f32[2,3,42,1,256]{4,0,1,3,2:T(2,128)S(1)} %get-tuple-element.58), channel_id=1, source_target_pairs={{0,2},{2,4},{4,6},{6,8},{8,10},{10,12},{12,14},{14,16},{16,18},{18... | collective-permute-start | bytes 774152 | tf_op jit(solution)/shard_map/ppermute | solution.py:20
  40.2 3.8 %collective-permute-start.4 = (f32[2,3,42,1,256]{4,0,1,3,2:T(2,128)S(1)}, f32[2,3,42,1,256]{4,0,1,3,2:T(2,128)S(1)}, u32[]{:S(2)}, u32[]{:S(2)}) collective-permute-start(f32[2,3,42,1,256]{4,0,1,3,2:T(2,128)S(1)} %get-tuple-element.59), channel_id=1, source_target_pairs={{2,0},{4,2},{6,4},{8,6},{10,8},{12,10},{14,12},{16,14},{18,16},{20... | collective-permute-start | bytes 774152 | tf_op jit(solution)/shard_map/ppermute | solution.py:22
  43.9 4.1 %fusion.8 = (f32[2,3,82,3,129]{4,0,1,3,2:T(2,128)S(1)}, f32[2,3,82,3,129]{4,0,1,3,2:T(2,128)S(1)}) fusion(f32[2,3,1,1,128]{4,0,1,3,2:T(2,128)S(1)} %broadcast.88, f32[2,3,82,3,1]{4,0,1,3,2:T(2,128)S(1)} %copy.153, f32[2,3,82,1,128]{4,0,1,3,2:T(2,128)S(1)} %collective-permute-done.1, f32[2,3,80,1,128]{4,0,1,3,2:T(2,128)S(1)} %copy.149, ...), kind=kLoop, calls=%fused_computation.16 | loop fusion | flops 1904040 | bytes 2290752 | tf_op jit(solution)/shard_map/concatenate | solution.py:18
  48.1 1.7 %fusion.59 = (f32[2,3,80,1,128]{4,0,1,3,2:T(2,128)S(1)}, f32[2,3,80,1,128]{4,0,1,3,2:T(2,128)S(1)}, f32[2,3,80,1,128]{4,0,1,3,2:T(2,128)S(1)}, f32[2,3,80,1,128]{4,0,1,3,2:T(2,128)S(1)}, f32[2,3,80,1,128]{4,0,1,3,2:T(2,128)S(1)}) fusion(f32[2,3,82,3,129]{4,0,1,3,2:T(2,128)S(1)} %get-tuple-element.49, f32[2,3,82,3,129]{4,0,1,3,2:T(2,128)S(1)} %get-tuple-element.48, ...), kind=kLoop, calls=%fused_computation.133 | loop fusion | flops 1413120 | bytes 5406720 | tf_op jit(solution)/shard_map/mul | solution.py:51
  49.8 1.1 slice_add_fusion.34
  52.0 0.7 fusion.100
  52.7 1.4 collective-permute-start.6
  54.1 4.8 %collective-permute-start.7 = (f32[2,3,42,4,1]{4,0,1,3,2:T(2,128)S(1)}, f32[2,3,42,4,1]{4,0,1,3,2:T(2,128)S(1)}, u32[]{:S(2)}, u32[]{:S(2)}) collective-permute-start(f32[2,3,42,4,1]{4,0,1,3,2:T(2,128)S(1)} %get-tuple-element.43), channel_id=1, source_target_pairs={{0,1},{2,3},{4,5},{6,7},{8,9},{10,11},{12,13},{14,15},{16,17},{18,... | collective-permute-start | bytes 12104 | tf_op jit(solution)/shard_map/ppermute | solution.py:20
  58.9 0.7 pad_maximum_fusion.10
  59.7 1.7 %slice_add_fusion.5 = (f32[2,3,40,2,256]{4,0,1,3,2:T(2,128)S(1)}, f32[2,3,40,2,256]{4,0,1,3,2:T(2,128)S(1)}, f32[2,3,40,2,256]{4,0,1,3,2:T(2,128)S(1)}) fusion(f32[2,3,42,3,256]{4,0,1,3,2:T(2,128)S(1)} %get-tuple-element.57, f32[2,3,42,3,256]{4,0,1,3,2:T(2,128)S(1)} %get-tuple-element.56, f32[2,3,40,2,256]{4,3,2,1,0:T(2,128)S(1)} %copy-done, ...), kind=kLoop, calls=%fused_computation.70 | loop fusion | flops 1843200 | bytes 5437440 | tf_op jit(solution)/shard_map/add | solution.py:46
  61.3 7.9 %collective-permute-done.6 = f32[2,3,42,4,1]{4,0,1,3,2:T(2,128)S(1)} collective-permute-done((f32[2,3,42,4,1]{4,0,1,3,2:T(2,128)S(1)}, f32[2,3,42,4,1]{4,0,1,3,2:T(2,128)S(1)}, u32[]{:S(2)}, u32[]{:S(2)}) %collective-permute-start.6) | collective-permute-done | bytes 4064 | tf_op jit(solution)/shard_map/ppermute | solution.py:22
  69.3 1.2 collective-permute-done.7
  70.5 3.7 %pad_maximum_fusion.4 = (f32[2,3,42,4,257]{4,0,1,3,2:T(2,128)S(1)}, f32[2,3,42,4,257]{4,0,1,3,2:T(2,128)S(1)}) fusion(f32[2,3,42,4,1]{4,0,1,3,2:T(2,128)S(1)} %collective-permute-done.6, f32[2,3,42,1,256]{4,0,1,3,2:T(2,128)S(1)} %collective-permute-done.4, f32[2,3,1,2,256]{4,0,1,3,2:T(2,128)S(1)} %reshape.216, f32[2,3,40,2,256]{4,0,1,3,2:T(2,128)S(1)} %copy.145, ...), kind=kLoop, calls=%fused_computation.4 | loop fusion | flops 2590560 | bytes 3112704 | tf_op jit(solution)/shard_map/concatenate | solution.py:18
  74.2 2.8 %fusion.20 = (f32[2,3,40,2,256]{4,0,1,3,2:T(2,128)S(1)}, f32[2,3,40,2,256]{4,0,1,3,2:T(2,128)S(1)}, f32[2,3,40,2,256]{4,0,1,3,2:T(2,128)S(1)}) fusion(f32[2,3,42,4,257]{4,0,1,3,2:T(2,128)S(1)} %get-tuple-element.41, f32[2,3,42,4,257]{4,0,1,3,2:T(2,128)S(1)} %get-tuple-element.40, f32[2,256]{1,0:T(2,128)S(1)} %get-tuple-element.92, ...), kind=kLoop, calls=%fused_computation.60 | loop fusion | flops 1597440 | bytes 6885376 | tf_op jit(solution)/shard_map/mul | solution.py:51
  77.4 0.7 copy-done.6
  78.1 1.5 fusion.26
  80.2 1.9 %collective-permute-start.13 = (f32[2,3,82,1,128]{4,0,1,3,2:T(2,128)S(1)}, f32[2,3,82,1,128]{4,0,1,3,2:T(2,128)S(1)}, u32[]{:S(2)}, u32[]{:S(2)}) collective-permute-start(f32[2,3,82,1,128]{4,0,1,3,2:T(2,128)S(1)} %pad_maximum_fusion.18), channel_id=1, source_target_pairs={{2,0},{4,2},{6,4},{8,6},{10,8},{12,10},{14,12},{16,14},{18,16},{20... | collective-permute-start | bytes 755720 | tf_op jit(solution)/shard_map/ppermute | solution.py:22
  82.1 2.4 %collective-permute-start.12 = (f32[2,3,82,1,128]{4,0,1,3,2:T(2,128)S(1)}, f32[2,3,82,1,128]{4,0,1,3,2:T(2,128)S(1)}, u32[]{:S(2)}, u32[]{:S(2)}) collective-permute-start(f32[2,3,82,1,128]{4,0,1,3,2:T(2,128)S(1)} %pad_maximum_fusion.18), channel_id=1, source_target_pairs={{0,2},{2,4},{4,6},{6,8},{8,10},{10,12},{12,14},{14,16},{16,18},{18... | collective-permute-start | bytes 755720 | tf_op jit(solution)/shard_map/ppermute | solution.py:20
  84.5 0.9 fusion.70
  85.4 0.9 fusion.39
  86.3 5.1 %collective-permute-done.12 = f32[2,3,82,1,128]{4,0,1,3,2:T(2,128)S(1)} collective-permute-done((f32[2,3,82,1,128]{4,0,1,3,2:T(2,128)S(1)}, f32[2,3,82,1,128]{4,0,1,3,2:T(2,128)S(1)}, u32[]{:S(2)}, u32[]{:S(2)}) %collective-permute-start.12) | collective-permute-done | bytes 251936 | tf_op jit(solution)/shard_map/ppermute | solution.py:20
  91.7 1.0 fusion.101
  92.7 1.1 copy.167
  94.3 1.3 collective-permute-start.15
  95.7 5.1 %collective-permute-start.14 = (f32[2,3,82,3,1]{2,3,4,1,0:T(4,128)}, f32[2,3,82,3,1]{2,3,4,1,0:T(4,128)S(1)}, u32[]{:S(2)}, u32[]{:S(2)}) collective-permute-start(f32[2,3,82,3,1]{2,3,4,1,0:T(4,128)} %copy.167), channel_id=1, source_target_pairs={{0,1},{2,3},{4,5},{6,7},{8,9},{10,11},{12,13},{14,15},{16,17},{18,... | collective-permute-start | bytes 17720 | tf_op jit(solution)/shard_map/ppermute | solution.py:20
  100.8 1.1 fusion.68
  102.9 1.2 copy.170
  104.3 1.2 copy.187
  105.5 1.6 %reshape.217 = f32[2,3,1,2,256]{4,0,1,3,2:T(2,128)S(1)} reshape(f32[2,3,2,128,2]{4,3,0,1,2:T(8,128)} %copy.187) | data formatting | bytes 24576 | tf_op jit(solution)/shard_map/broadcast_in_dim;reshape | solution.py:126
  107.5 1.9 %collective-permute-start.17 = (f32[2,3,42,1,256]{4,0,1,3,2:T(2,128)S(1)}, f32[2,3,42,1,256]{4,0,1,3,2:T(2,128)S(1)}, u32[]{:S(2)}, u32[]{:S(2)}) collective-permute-start(f32[2,3,42,1,256]{4,0,1,3,2:T(2,128)S(1)} %get-tuple-element.54), channel_id=1, source_target_pairs={{0,2},{2,4},{4,6},{6,8},{8,10},{10,12},{12,14},{14,16},{16,18},{18... | collective-permute-start | bytes 774152 | tf_op jit(solution)/shard_map/ppermute | solution.py:20
  109.4 3.9 %collective-permute-start.16 = (f32[2,3,42,1,256]{4,0,1,3,2:T(2,128)S(1)}, f32[2,3,42,1,256]{4,0,1,3,2:T(2,128)S(1)}, u32[]{:S(2)}, u32[]{:S(2)}) collective-permute-start(f32[2,3,42,1,256]{4,0,1,3,2:T(2,128)S(1)} %get-tuple-element.55), channel_id=1, source_target_pairs={{2,0},{4,2},{6,4},{8,6},{10,8},{12,10},{14,12},{16,14},{18,16},{20... | collective-permute-start | bytes 774152 | tf_op jit(solution)/shard_map/ppermute | solution.py:22
  113.3 4.1 %fusion.11 = (f32[2,3,82,3,129]{4,0,1,3,2:T(2,128)S(1)}, f32[2,3,82,3,129]{4,0,1,3,2:T(2,128)S(1)}) fusion(f32[2,3,1,1,128]{4,0,1,3,2:T(2,128)S(1)} %broadcast.88, f32[2,3,82,3,1]{4,0,1,3,2:T(2,128)S(1)} %copy.170, f32[2,3,82,1,128]{4,0,1,3,2:T(2,128)S(1)} %collective-permute-done.13, f32[2,3,80,1,128]{4,0,1,3,2:T(2,128)S(1)} %fusion.64, ...), kind=kLoop, calls=%fused_computation.19 | loop fusion | flops 1904040 | bytes 2290752 | tf_op jit(solution)/shard_map/concatenate | solution.py:18
  117.5 1.7 %fusion.48 = (f32[2,3,80,1,128]{4,0,1,3,2:T(2,128)S(1)}, f32[2,3,80,1,128]{4,0,1,3,2:T(2,128)S(1)}, f32[2,3,80,1,128]{4,0,1,3,2:T(2,128)S(1)}, f32[2,3,80,1,128]{4,0,1,3,2:T(2,128)S(1)}, f32[2,3,80,1,128]{4,0,1,3,2:T(2,128)S(1)}) fusion(f32[2,3,82,3,129]{4,0,1,3,2:T(2,128)S(1)} %get-tuple-element.45, f32[2,3,82,3,129]{4,0,1,3,2:T(2,128)S(1)} %get-tuple-element.44, ...), kind=kLoop, calls=%fused_computation.110 | loop fusion | flops 1413120 | bytes 5406720 | tf_op jit(solution)/shard_map/mul | solution.py:51
  119.2 1.1 slice_add_fusion.28
  120.8 0.9 copy.183
  122.0 0.6 add.360
  123.1 0.7 fusion.99
  123.8 1.3 collective-permute-start.18
  125.1 4.6 %collective-permute-start.19 = (f32[2,3,42,4,1]{4,0,1,3,2:T(2,128)S(1)}, f32[2,3,42,4,1]{4,0,1,3,2:T(2,128)S(1)}, u32[]{:S(2)}, u32[]{:S(2)}) collective-permute-start(f32[2,3,42,4,1]{4,0,1,3,2:T(2,128)S(1)} %get-tuple-element.39), channel_id=1, source_target_pairs={{0,1},{2,3},{4,5},{6,7},{8,9},{10,11},{12,13},{14,15},{16,17},{18,... | collective-permute-start | bytes 12104 | tf_op jit(solution)/shard_map/ppermute | solution.py:20
  129.7 0.7 pad_maximum_fusion.11
  130.5 0.6 slice_add_fusion.2
  131.1 8.2 %collective-permute-done.18 = f32[2,3,42,4,1]{4,0,1,3,2:T(2,128)S(1)} collective-permute-done((f32[2,3,42,4,1]{4,0,1,3,2:T(2,128)S(1)}, f32[2,3,42,4,1]{4,0,1,3,2:T(2,128)S(1)}, u32[]{:S(2)}, u32[]{:S(2)}) %collective-permute-start.18) | collective-permute-done | bytes 4064 | tf_op jit(solution)/shard_map/ppermute | solution.py:22
  139.3 1.2 collective-permute-done.19
  140.5 3.7 %pad_maximum_fusion.5 = (f32[2,3,42,4,257]{4,0,1,3,2:T(2,128)S(1)}, f32[2,3,42,4,257]{4,0,1,3,2:T(2,128)S(1)}) fusion(f32[2,3,42,4,1]{4,0,1,3,2:T(2,128)S(1)} %collective-permute-done.18, f32[2,3,42,1,256]{4,0,1,3,2:T(2,128)S(1)} %collective-permute-done.16, f32[2,3,1,2,256]{4,0,1,3,2:T(2,128)S(1)} %reshape.217, f32[2,3,40,2,256]{4,0,1,3,2:T(2,128)S(1)} %fusion.26, ...), kind=kLoop, calls=%fused_computation.6 | loop fusion | flops 2590560 | bytes 3112704 | tf_op jit(solution)/shard_map/concatenate | solution.py:18
  144.2 3.0 %fusion.16 = (f32[2,3,40,2,256]{4,0,1,3,2:T(2,128)S(1)}, f32[2,3,40,2,256]{4,0,1,3,2:T(2,128)S(1)}, f32[2,3,40,2,256]{4,0,1,3,2:T(2,128)S(1)}, f32[2,3,40,2,256]{4,0,1,3,2:T(2,128)S(1)}) fusion(f32[2,3,42,4,257]{4,0,1,3,2:T(2,128)S(1)} %get-tuple-element.37, f32[2,3,42,4,257]{4,0,1,3,2:T(2,128)S(1)} %get-tuple-element.36, ...), kind=kLoop, calls=%fused_computation.43 | loop fusion | flops 2211840 | bytes 7403520 | tf_op jit(solution)/shard_map/mul | solution.py:51
  148.2 1.2 fusion.29
  149.9 1.0 copy.182
  150.9 0.7 add.359
  (98 shorter events, 11.0 us)
Async XLA Ops:
  0.6 7.6 %copy-start.16 = (s32[2,256]{1,0:T(2,128)S(1)}, s32[2,256]{1,0:T(2,128)}, u32[]{:S(2)}) copy-start(s32[2,256]{1,0:T(2,128)} %param.17) | copy-start | bytes 6148
  0.6 14.3 %copy-start.7 = (f32[80,1,128]{2,1,0:T(1,128)S(1)}, f32[80,1,128]{2,1,0:T(1,128)}, u32[]{:S(2)}) copy-start(f32[80,1,128]{2,1,0:T(1,128)} %param.15) | copy-start | bytes 122884
  0.7 14.2 %copy-start.15 = (f32[80,1,128]{2,1,0:T(1,128)S(1)}, f32[80,1,128]{2,1,0:T(1,128)}, u32[]{:S(2)}) copy-start(f32[80,1,128]{2,1,0:T(1,128)} %param.16) | copy-start | bytes 122884
  0.7 14.3 %copy-start.2 = (f32[40,2,256]{2,1,0:T(2,128)S(1)}, f32[40,2,256]{2,1,0:T(2,128)}, u32[]{:S(2)}) copy-start(f32[40,2,256]{2,1,0:T(2,128)} %param.13) | copy-start | bytes 245764
  0.7 14.3 %copy-start.14 = (f32[40,2,256]{2,1,0:T(2,128)S(1)}, f32[40,2,256]{2,1,0:T(2,128)}, u32[]{:S(2)}) copy-start(f32[40,2,256]{2,1,0:T(2,128)} %param.14) | copy-start | bytes 245764
  3.9 20.5 %collective-permute-start.1 = (f32[2,3,82,1,128]{4,0,1,3,2:T(2,128)S(1)}, f32[2,3,82,1,128]{4,0,1,3,2:T(2,128)S(1)}, u32[]{:S(2)}, u32[]{:S(2)}) collective-permute-start(f32[2,3,82,1,128]{4,0,1,3,2:T(2,128)S(1)} %pad_maximum_fusion.19), channel_id=1, source_target_pairs={{2,0},{4,2},{6,4},{8,6},{10,8},{12,10},{14,12},{16,14},{18,16},{20... | collective-permute-start | bytes 755720 | tf_op jit(solution)/shard_map/ppermute | solution.py:22
  5.8 18.6 %collective-permute-start = (f32[2,3,82,1,128]{4,0,1,3,2:T(2,128)S(1)}, f32[2,3,82,1,128]{4,0,1,3,2:T(2,128)S(1)}, u32[]{:S(2)}, u32[]{:S(2)}) collective-permute-start(f32[2,3,82,1,128]{4,0,1,3,2:T(2,128)S(1)} %pad_maximum_fusion.19), channel_id=1, source_target_pairs={{0,2},{2,4},{4,6},{6,8},{8,10},{10,12},{12,14},{14,16},{16,18},{18... | collective-permute-start | bytes 755720 | tf_op jit(solution)/shard_map/ppermute | solution.py:20
  8.2 6.9 %collective-permute-start.8 = (s32[1,256]{1,0:T(1,128)S(1)}, s32[1,256]{1,0:T(1,128)S(1)}, u32[]{:S(2)}, u32[]{:S(2)}) collective-permute-start(s32[1,256]{1,0:T(1,128)S(1)} %get-tuple-element.98), channel_id=1, source_target_pairs={{0,2},{2,4},{4,6},{6,8},{8,10},{10,12},{12,14},{14,16},{16,18},{18... | collective-permute-start | bytes 3080 | tf_op jit(solution)/shard_map/ppermute | solution.py:20
  12.1 3.2 %collective-permute-start.9 = (s32[1,256]{1,0:T(1,128)S(1)}, s32[1,256]{1,0:T(1,128)S(1)}, u32[]{:S(2)}, u32[]{:S(2)}) collective-permute-start(s32[1,256]{1,0:T(1,128)S(1)} %get-tuple-element.99), channel_id=1, source_target_pairs={{2,0},{4,2},{6,4},{8,6},{10,8},{12,10},{14,12},{16,14},{18,16},{20... | collective-permute-start | bytes 3080 | tf_op jit(solution)/shard_map/ppermute | solution.py:22
  15.0 35.9 %copy-start.9 = (f32[80,1,128]{2,1,0:T(1,128)}, f32[80,1,128]{2,1,0:T(1,128)S(1)}, u32[]{:S(2)}) copy-start(f32[80,1,128]{2,1,0:T(1,128)S(1)} %add.317) | copy-start | bytes 122884
  15.0 62.4 %copy-start.4 = (f32[40,2,256]{2,1,0:T(2,128)}, f32[40,2,256]{2,1,0:T(2,128)S(1)}, u32[]{:S(2)}) copy-start(f32[40,2,256]{2,1,0:T(2,128)S(1)} %add.300) | copy-start | bytes 245764
  15.4 4.7 %collective-permute-start.10 = (s32[4,1]{1,0:T(4,128)S(1)}, s32[4,1]{1,0:T(4,128)S(1)}, u32[]{:S(2)}, u32[]{:S(2)}) collective-permute-start(s32[4,1]{1,0:T(4,128)S(1)} %get-tuple-element.96), channel_id=1, source_target_pairs={{0,1},{2,3},{4,5},{6,7},{8,9},{10,11},{12,13},{14,15},{16,17},{18,... | collective-permute-start | bytes 56 | tf_op jit(solution)/shard_map/ppermute | solution.py:20
  18.8 5.5 %collective-permute-start.11 = (s32[4,1]{1,0:T(4,128)S(1)}, s32[4,1]{1,0:T(4,128)S(1)}, u32[]{:S(2)}, u32[]{:S(2)}) collective-permute-start(s32[4,1]{1,0:T(4,128)S(1)} %get-tuple-element.97), channel_id=1, source_target_pairs={{1,0},{3,2},{5,4},{7,6},{9,8},{11,10},{13,12},{15,14},{17,16},{19,... | collective-permute-start | bytes 56 | tf_op jit(solution)/shard_map/ppermute | solution.py:22
  26.6 7.7 %collective-permute-start.3 = (f32[2,3,82,3,1]{2,0,4,3,1:T(2,128)S(1)}, f32[2,3,82,3,1]{2,0,4,3,1:T(2,128)S(1)}, u32[]{:S(2)}, u32[]{:S(2)}) collective-permute-start(f32[2,3,82,3,1]{2,0,4,3,1:T(2,128)S(1)} %copy.151), channel_id=1, source_target_pairs={{1,0},{3,2},{5,4},{7,6},{9,8},{11,10},{13,12},{15,14},{17,16},{19,... | collective-permute-start | bytes 17720 | tf_op jit(solution)/shard_map/ppermute | solution.py:22
  27.9 5.9 %collective-permute-start.2 = (f32[2,3,82,3,1]{2,0,4,3,1:T(2,128)S(1)}, f32[2,3,82,3,1]{2,0,4,3,1:T(2,128)S(1)}, u32[]{:S(2)}, u32[]{:S(2)}) collective-permute-start(f32[2,3,82,3,1]{2,0,4,3,1:T(2,128)S(1)} %copy.150), channel_id=1, source_target_pairs={{0,1},{2,3},{4,5},{6,7},{8,9},{10,11},{12,13},{14,15},{16,17},{18,... | collective-permute-start | bytes 17720 | tf_op jit(solution)/shard_map/ppermute | solution.py:20
  38.2 13.3 %collective-permute-start.5 = (f32[2,3,42,1,256]{4,0,1,3,2:T(2,128)S(1)}, f32[2,3,42,1,256]{4,0,1,3,2:T(2,128)S(1)}, u32[]{:S(2)}, u32[]{:S(2)}) collective-permute-start(f32[2,3,42,1,256]{4,0,1,3,2:T(2,128)S(1)} %get-tuple-element.58), channel_id=1, source_target_pairs={{0,2},{2,4},{4,6},{6,8},{8,10},{10,12},{12,14},{14,16},{16,18},{18... | collective-permute-start | bytes 774152 | tf_op jit(solution)/shard_map/ppermute | solution.py:20
  40.2 7.9 %copy-start.1 = (f32[2,3,80,1,128]{4,3,2,1,0:T(1,128)S(1)}, f32[2,3,80,1,128]{4,3,2,1,0:T(1,128)}, u32[]{:S(2)}) copy-start(f32[2,3,80,1,128]{4,3,2,1,0:T(1,128)} %param.12) | copy-start | bytes 737284
  40.2 11.3 %collective-permute-start.4 = (f32[2,3,42,1,256]{4,0,1,3,2:T(2,128)S(1)}, f32[2,3,42,1,256]{4,0,1,3,2:T(2,128)S(1)}, u32[]{:S(2)}, u32[]{:S(2)}) collective-permute-start(f32[2,3,42,1,256]{4,0,1,3,2:T(2,128)S(1)} %get-tuple-element.59), channel_id=1, source_target_pairs={{2,0},{4,2},{6,4},{8,6},{10,8},{12,10},{14,12},{16,14},{18,16},{20... | collective-permute-start | bytes 774152 | tf_op jit(solution)/shard_map/ppermute | solution.py:22
  48.1 2.8 %copy-start.12 = (f32[2,3,80,1,128]{4,3,2,1,0:T(1,128)S(1)}, f32[2,3,80,1,128]{4,3,2,1,0:T(1,128)}, u32[]{:S(2)}) copy-start(f32[2,3,80,1,128]{4,3,2,1,0:T(1,128)} %param.11) | copy-start | bytes 737284
  52.7 7.0 %copy-start = (f32[2,3,40,2,256]{4,3,2,1,0:T(2,128)S(1)}, f32[2,3,40,2,256]{4,3,2,1,0:T(2,128)}, u32[]{:S(2)}) copy-start(f32[2,3,40,2,256]{4,3,2,1,0:T(2,128)} %param.10) | copy-start | bytes 1474564
  52.7 16.6 %collective-permute-start.6 = (f32[2,3,42,4,1]{4,0,1,3,2:T(2,128)S(1)}, f32[2,3,42,4,1]{4,0,1,3,2:T(2,128)S(1)}, u32[]{:S(2)}, u32[]{:S(2)}) collective-permute-start(f32[2,3,42,4,1]{4,0,1,3,2:T(2,128)S(1)} %get-tuple-element.42), channel_id=1, source_target_pairs={{1,0},{3,2},{5,4},{7,6},{9,8},{11,10},{13,12},{15,14},{17,16},{19,... | collective-permute-start | bytes 12104 | tf_op jit(solution)/shard_map/ppermute | solution.py:22
  54.1 16.4 %collective-permute-start.7 = (f32[2,3,42,4,1]{4,0,1,3,2:T(2,128)S(1)}, f32[2,3,42,4,1]{4,0,1,3,2:T(2,128)S(1)}, u32[]{:S(2)}, u32[]{:S(2)}) collective-permute-start(f32[2,3,42,4,1]{4,0,1,3,2:T(2,128)S(1)} %get-tuple-element.43), channel_id=1, source_target_pairs={{0,1},{2,3},{4,5},{6,7},{8,9},{10,11},{12,13},{14,15},{16,17},{18,... | collective-permute-start | bytes 12104 | tf_op jit(solution)/shard_map/ppermute | solution.py:20
  77.0 1.0 copy-start.6
  80.2 6.1 %collective-permute-start.13 = (f32[2,3,82,1,128]{4,0,1,3,2:T(2,128)S(1)}, f32[2,3,82,1,128]{4,0,1,3,2:T(2,128)S(1)}, u32[]{:S(2)}, u32[]{:S(2)}) collective-permute-start(f32[2,3,82,1,128]{4,0,1,3,2:T(2,128)S(1)} %pad_maximum_fusion.18), channel_id=1, source_target_pairs={{2,0},{4,2},{6,4},{8,6},{10,8},{12,10},{14,12},{16,14},{18,16},{20... | collective-permute-start | bytes 755720 | tf_op jit(solution)/shard_map/ppermute | solution.py:22
  82.1 9.2 %collective-permute-start.12 = (f32[2,3,82,1,128]{4,0,1,3,2:T(2,128)S(1)}, f32[2,3,82,1,128]{4,0,1,3,2:T(2,128)S(1)}, u32[]{:S(2)}, u32[]{:S(2)}) collective-permute-start(f32[2,3,82,1,128]{4,0,1,3,2:T(2,128)S(1)} %pad_maximum_fusion.18), channel_id=1, source_target_pairs={{0,2},{2,4},{4,6},{6,8},{8,10},{10,12},{12,14},{14,16},{16,18},{18... | collective-permute-start | bytes 755720 | tf_op jit(solution)/shard_map/ppermute | solution.py:20
  94.3 8.5 %collective-permute-start.15 = (f32[2,3,82,3,1]{2,3,4,1,0:T(4,128)S(1)}, f32[2,3,82,3,1]{2,3,4,1,0:T(4,128)}, u32[]{:S(2)}, u32[]{:S(2)}) collective-permute-start(f32[2,3,82,3,1]{2,3,4,1,0:T(4,128)S(1)} %copy.168), channel_id=1, source_target_pairs={{1,0},{3,2},{5,4},{7,6},{9,8},{11,10},{13,12},{15,14},{17,16},{19,... | collective-permute-start | bytes 17720 | tf_op jit(solution)/shard_map/ppermute | solution.py:22
  95.7 6.7 %collective-permute-start.14 = (f32[2,3,82,3,1]{2,3,4,1,0:T(4,128)}, f32[2,3,82,3,1]{2,3,4,1,0:T(4,128)S(1)}, u32[]{:S(2)}, u32[]{:S(2)}) collective-permute-start(f32[2,3,82,3,1]{2,3,4,1,0:T(4,128)} %copy.167), channel_id=1, source_target_pairs={{0,1},{2,3},{4,5},{6,7},{8,9},{10,11},{12,13},{14,15},{16,17},{18,... | collective-permute-start | bytes 17720 | tf_op jit(solution)/shard_map/ppermute | solution.py:20
  107.5 15.1 %collective-permute-start.17 = (f32[2,3,42,1,256]{4,0,1,3,2:T(2,128)S(1)}, f32[2,3,42,1,256]{4,0,1,3,2:T(2,128)S(1)}, u32[]{:S(2)}, u32[]{:S(2)}) collective-permute-start(f32[2,3,42,1,256]{4,0,1,3,2:T(2,128)S(1)} %get-tuple-element.54), channel_id=1, source_target_pairs={{0,2},{2,4},{4,6},{6,8},{8,10},{10,12},{12,14},{14,16},{16,18},{18... | collective-permute-start | bytes 774152 | tf_op jit(solution)/shard_map/ppermute | solution.py:20
  109.4 13.2 %collective-permute-start.16 = (f32[2,3,42,1,256]{4,0,1,3,2:T(2,128)S(1)}, f32[2,3,42,1,256]{4,0,1,3,2:T(2,128)S(1)}, u32[]{:S(2)}, u32[]{:S(2)}) collective-permute-start(f32[2,3,42,1,256]{4,0,1,3,2:T(2,128)S(1)} %get-tuple-element.55), channel_id=1, source_target_pairs={{2,0},{4,2},{6,4},{8,6},{10,8},{12,10},{14,12},{16,14},{18,16},{20... | collective-permute-start | bytes 774152 | tf_op jit(solution)/shard_map/ppermute | solution.py:22
  117.4 2.8 %copy-start.8 = (f32[80,1,128]{2,1,0:T(1,128)S(1)}, f32[80,1,128]{2,1,0:T(1,128)}, u32[]{:S(2)}) copy-start(f32[80,1,128]{2,1,0:T(1,128)} %param.15) | copy-start | bytes 122884
  117.4 2.8 %copy-start.10 = (f32[80,1,128]{2,1,0:T(1,128)S(1)}, f32[80,1,128]{2,1,0:T(1,128)}, u32[]{:S(2)}) copy-start(f32[80,1,128]{2,1,0:T(1,128)} %copy-done.9) | copy-start | bytes 122884
  119.2 2.8 %copy-start.13 = (f32[80,128]{1,0:T(8,128)S(1)}, f32[80,128]{1,0:T(8,128)}, u32[]{:S(2)}) copy-start(f32[80,128]{1,0:T(8,128)} %fusion.70) | copy-start | bytes 122884
  123.8 15.5 %collective-permute-start.18 = (f32[2,3,42,4,1]{4,0,1,3,2:T(2,128)S(1)}, f32[2,3,42,4,1]{4,0,1,3,2:T(2,128)S(1)}, u32[]{:S(2)}, u32[]{:S(2)}) collective-permute-start(f32[2,3,42,4,1]{4,0,1,3,2:T(2,128)S(1)} %get-tuple-element.38), channel_id=1, source_target_pairs={{1,0},{3,2},{5,4},{7,6},{9,8},{11,10},{13,12},{15,14},{17,16},{19,... | collective-permute-start | bytes 12104 | tf_op jit(solution)/shard_map/ppermute | solution.py:22
  125.1 15.4 %collective-permute-start.19 = (f32[2,3,42,4,1]{4,0,1,3,2:T(2,128)S(1)}, f32[2,3,42,4,1]{4,0,1,3,2:T(2,128)S(1)}, u32[]{:S(2)}, u32[]{:S(2)}) collective-permute-start(f32[2,3,42,4,1]{4,0,1,3,2:T(2,128)S(1)} %get-tuple-element.39), channel_id=1, source_target_pairs={{0,1},{2,3},{4,5},{6,7},{8,9},{10,11},{12,13},{14,15},{16,17},{18,... | collective-permute-start | bytes 12104 | tf_op jit(solution)/shard_map/ppermute | solution.py:20
  147.2 0.9 copy-start.3
  147.2 0.9 copy-start.5
  149.4 1.6 %copy-start.11 = (f32[40,2,256]{2,1,0:T(2,128)S(1)}, f32[40,2,256]{2,1,0:T(2,128)}, u32[]{:S(2)}) copy-start(f32[40,2,256]{2,1,0:T(2,128)} %fusion.68) | copy-start | bytes 245764
where the time goes:
time: 153 us; the launch traced here: 152 us
  starting transfers between devices  55 us (36%)
  other arithmetic  44 us (29%)
  waiting for transfers between devices  29.9 us (20%)
  local copies, waits for them, and re-layouts  21.3 us (14%)
    ppermute x10, starting transfers between devices, with_halo(): lax.ppermute(tail, axis, [(i, (i + 1) % count) for i in range(ends)])  35 us
    ppermute x10, waiting for transfers between devices, with_halo(): lax.ppermute(head, axis, [((i + 1) % count, i) for i in range(ends)])  20.5 us
    ppermute x10, starting transfers between devices, with_halo(): lax.ppermute(head, axis, [((i + 1) % count, i) for i in range(ends)])  20 us
    concatenate x12, other arithmetic, with_halo(): jnp.concatenate([lax.ppermute(tail, axis, [(i, (i + 1) % count) for i in...  18.8 us
    ppermute x10, waiting for transfers between devices, with_halo(): lax.ppermute(tail, axis, [(i, (i + 1) % count) for i in range(ends)])  9.31 us
    mul x4, other arithmetic, accelerate(): (offset(padded, 0, 1, 1) - offset(padded, 0, 1, -1) - offset(padded, 0, -...  9.22 us
    unnamed x38, local copies, waits for them, and re-layouts  5.83 us
    another operation x4, local copies, waits for them, and re-layouts, on_device(): ghost[:, :, None]  5.59 us
  transfers between devices with their start and end apart: 20, of which 10 were waited for; matrix products, arithmetic and copies ran while one was open for 17% of the time, Pallas kernels for 0%

commit v1 on v0

v1 whole, which is shorter than its diff:
```python
import functools

import jax
import jax.numpy as jnp
from jax import lax
from jax.experimental import pallas as pl
from jax.experimental.pallas import tpu as pltpu
from jax.sharding import PartitionSpec as P

STEPS = 2
STEP_SQUARED = 0.04
LANES = 128
HALF = LANES // 2
TOP = 8


def stencil(ext, s, depth, own, grid_step, half_inv, inv_sq):
    total = ext.shape[-1]
    inverse_area = 1.0 / (grid_step * grid_step)
    tilt = 0.5 / grid_step

    def rows(slot, c, shift):
        return ext[slot, c, TOP + shift : TOP + shift + depth, :]

    def across(v):
        return pltpu.roll(v, total - 1, 1)[:, :own] - pltpu.roll(v, 1, 1)[:, :own]

    xx, yy, zz, mxy, mxz, myz = [], [], [], {}, {}, {}
    for c in range(3):
        wide = rows(s, c, 0)
        mid = wide[:, :own]
        east, west = rows(s + 1, c, 0), rows(s - 1, c, 0)
        down, up = rows(s, c, 1), rows(s, c, -1)
        twice = 2.0 * mid
        xx.append((east[:, :own] - twice + west[:, :own]) * inverse_area)
        yy.append(
            (pltpu.roll(wide, total - 1, 1)[:, :own] - twice + pltpu.roll(wide, 1, 1)[:, :own])
            * inverse_area
        )
        zz.append((down[:, :own] - twice + up[:, :own]) * inv_sq[s][:, :own])
        if c != 2:
            mxy[c] = across(east - west) * (0.25 * inverse_area)
        if c != 1:
            e = (rows(s + 1, c, 1) - rows(s + 1, c, -1))[:, :own] * half_inv[s + 1][:, :own]
            w = (rows(s - 1, c, 1) - rows(s - 1, c, -1))[:, :own] * half_inv[s - 1][:, :own]
            mxz[c] = (e - w) * tilt
        if c != 0:
            myz[c] = across((down - up) * half_inv[s]) * tilt
    laplace = [xx[c] + yy[c] + zz[c] for c in range(3)]
    grad_div = [
        xx[0] + mxy[1] + mxz[2],
        mxy[0] + yy[1] + myz[2],
        mxz[0] + myz[1] + zz[2],
    ]
    return laplace, grad_div


def body(
    nx, ny, fz, cz, fy, cy,
    fold, fnow, cold, cnow, shf, laf, shc, lac, topo,
    fout, cout, fker, cker,
    fn, cn, xf, xc, xg, pk, yr, mg, jown, jx, ext, extc, ghin, ghost,
    xs, xr, gs, gr, ys, yrs, js, jr,
):
    gx, gy = lax.axis_index("gx"), lax.axis_index("gy")
    has_x = (gx > 0, gx < nx - 1)
    has_y = (gy > 0, gy < ny - 1)
    tiles = fy // LANES
    rows_c = cn.shape[2]

    barrier = pltpu.get_barrier_semaphore()
    for side in range(2):
        step = 2 * side - 1

        @pl.when(has_x[side])
        def _():
            pl.semaphore_signal(barrier, inc=1, device_id={"gx": gx + step})

        @pl.when(has_y[side])
        def _():
            pl.semaphore_signal(barrier, inc=1, device_id={"gy": gy + step})

        @pl.when(jnp.logical_not(has_x[side]))
        def _():
            xf[:, side] = jnp.zeros(xf.shape[:1] + xf.shape[2:], jnp.float32)
            xc[:, side] = jnp.zeros(xc.shape[:1] + xc.shape[2:], jnp.float32)
            xg[:, side] = jnp.zeros(xg.shape[:1] + xg.shape[2:], jnp.float32)
            jx[side] = jnp.ones(jx.shape[1:], jnp.float32)

        @pl.when(jnp.logical_not(has_y[side]))
        def _():
            yr[:, side] = jnp.zeros(yr.shape[:1] + yr.shape[2:], jnp.float32)

    def x_copies(t, f, d):
        part = pl.ds(3 * f, 3)
        dev = {"gx": gx + 2 * d - 1}
        return (
            pltpu.make_async_remote_copy(
                cn.at[t, part], xc.at[t, 1 - d, part], xs.at[t, d, f, 0], xr.at[t, 1 - d, f, 0],
                device_id=dev,
            ),
            pltpu.make_async_remote_copy(
                fn.at[t, d, part], xf.at[t, 1 - d, part], xs.at[t, d, f, 1], xr.at[t, 1 - d, f, 1],
                device_id=dev,
            ),
        )

    def x_wait_copies(t, f, d):
        part = pl.ds(3 * f, 3)
        dev = {"gx": gx + 2 * d - 1}
        return (
            pltpu.make_async_remote_copy(
                cn.at[t, part], xc.at[t, d, part], xs.at[t, d, f, 0], xr.at[t, d, f, 0],
                device_id=dev,
            ),
            pltpu.make_async_remote_copy(
                fn.at[t, d, part], xf.at[t, d, part], xs.at[t, d, f, 1], xr.at[t, d, f, 1],
                device_id=dev,
            ),
        )

    def g_copy(t, d, land):
        return pltpu.make_async_remote_copy(
            mg.at[t], xg.at[t, land], gs.at[t, d], gr.at[t, land], device_id={"gx": gx + 2 * d - 1}
        )

    def y_copy(t, d, land):
        return pltpu.make_async_remote_copy(
            pk.at[t, d], yr.at[t, land], ys.at[t, d], yrs.at[t, land],
            device_id={"gy": gy + 2 * d - 1},
        )

    def j_copy(d, land):
        return pltpu.make_async_remote_copy(
            jown, jx.at[land], js.at[d], jr.at[land], device_id={"gx": gx + 2 * d - 1}
        )

    def each(flags, action):
        for d in range(2):
            pl.when(flags[d])(functools.partial(action, d))

    def send_x(t, f):
        def go(d):
            for copy in x_copies(t, f, d):
                copy.start()

        each(has_x, go)

    lane_f = lax.broadcasted_iota(jnp.int32, (fz, LANES), 1)
    lane_c = lax.broadcasted_iota(jnp.int32, (rows_c, LANES), 1)

    pair_row = lax.broadcasted_iota(jnp.int32, (fy, cy), 0)
    pair_col = lax.broadcasted_iota(jnp.int32, (fy, cy), 1)
    pairs = jnp.where(pair_row // 2 == pair_col, 0.25, 0.0).astype(jnp.float32)
    src = lax.broadcasted_iota(jnp.int32, (cy + LANES, fy + LANES), 0)
    dst = lax.broadcasted_iota(jnp.int32, (cy + LANES, fy + LANES), 1)
    src = jnp.where(src == cy + LANES - 1, -1, src)
    dst = jnp.where(dst == fy + LANES - 1, -1, dst)
    near = (dst + 2) // 2 - 1
    other = near + 2 * (dst + 2 - 2 * (near + 1)) - 1
    spread = jnp.where(src == near, 0.75, jnp.where(src == other, 0.25, 0.0)).astype(jnp.float32)

    def dot(a, b):
        return lax.dot_general(
            a, b, (((1,), (0,)), ((), ())),
            precision=lax.Precision.HIGHEST, preferred_element_type=jnp.float32,
        )

    def set_ridge(t, f):
        ghin[...] = jnp.zeros(ghin.shape, jnp.float32)
        for c in range(3):
            i = 3 * f + c
            ghin[c : c + 1, :fy] = fn[t, 0, i, fz - 1 : fz, :] + fn[t, 1, i, fz - 1 : fz, :]
        ridge = dot(ghin[0:8, :fy], pairs)
        for c in range(3):
            cn[t, 3 * f + c, cz : cz + 8, :] = jnp.broadcast_to(ridge[c : c + 1], (8, cy))

    jown[...] = jnp.ones(jown.shape, jnp.float32)
    jown[0:2, :] = 1.0 + topo[...].astype(jnp.float32) * (1.0 / 1024.0)
    for f in range(2):
        for i in range(3 * f, 3 * f + 3):
            cn[0, i, 0:cz, :] = cnow[i]
            for x in range(2):
                for y in range(tiles):
                    fn[0, x, i, :, y * LANES : (y + 1) * LANES] = fnow[
                        i, pl.ds(2 * y + x, fz, stride=2 * tiles), :
                    ]
        set_ridge(0, f)
    count = sum(h.astype(jnp.int32) for h in has_x + has_y)
    pl.semaphore_wait(barrier, count)
    each(has_x, lambda d: j_copy(d, 1 - d).start())
    send_x(0, 0)

    def pack(t):
        for d in range(2):
            base = HALF * (1 - d)
            at = (0, fy - 1)[d]
            fine = jnp.zeros((fz, LANES), jnp.float32)
            for i in range(6):
                for x in range(2):
                    fine = jnp.where(lane_f == base + 2 * i + x, fn[t, x, i, :, at : at + 1], fine)
            if t == 0:
                for x in range(2):
                    fine = jnp.where(
                        lane_f == base + 12 + x, jown[x : x + 1, at : at + 1], fine
                    )
            coarse = jnp.zeros((rows_c, LANES), jnp.float32)
            at = (0, cy - 1)[d]
            for i in range(6):
                coarse = jnp.where(lane_c == base + i, cn[t, i, :, at : at + 1], coarse)
            pk[t, d, 0:fz, :] = fine
            pk[t, d, fz : fz + rows_c, :] = coarse

    def exchange_columns(t):
        pack(t)
        each(has_y, lambda d: y_copy(t, d, 1 - d).start())
        each(has_y, lambda d: y_copy(t, d, d).wait_recv())
        low = lax.broadcasted_iota(jnp.int32, mg.shape[1:], 1) < HALF
        mg[t] = jnp.where(low, yr[t, 0], yr[t, 1])
        each(has_x, lambda d: g_copy(t, d, 1 - d).start())

    exchange_columns(0)
    send_x(0, 1)

    def halo_tile(v, k, lane):
        return jnp.where(
            lane == 0,
            v[:, HALF + k : HALF + k + 1],
            jnp.where(lane == LANES - 1, v[:, k : k + 1], 0.0),
        )

    each(has_x, lambda d: j_copy(d, d).wait_recv())
    lane_1 = lax.broadcasted_iota(jnp.int32, (1, LANES), 1)
    half_inv, inv_sq = {}, {}
    for q in range(4):
        if q in (0, 3):
            row = jx[0, 1:2, :] if q == 0 else jx[1, 0:1, :]
            edge = jnp.ones((1, LANES), jnp.float32)
        else:
            row = jown[q - 1 : q, :]
            head = mg[0, 0:8, :][0:1]
            edge = halo_tile(head, 12 + q - 1, lane_1)
            edge = jnp.where(edge == 0.0, 1.0, edge)
        row = jnp.concatenate([row, edge], axis=1)
        half_inv[q] = 0.5 / row
        inv_sq[q] = 1.0 / (row * row)
    half_c = {q: jnp.full((1, cy + LANES), 0.25, jnp.float32) for q in range(3)}
    sq_c = {q: jnp.full((1, cy + LANES), 0.25, jnp.float32) for q in range(3)}

    lane_g = lax.broadcasted_iota(jnp.int32, (16, fy + LANES), 1)
    row_g = lax.broadcasted_iota(jnp.int32, (16, fy + LANES), 0)
    keep = (lane_g < fy)
    keep = keep | ((lane_g == fy) & has_y[1]) | ((lane_g == fy + LANES - 1) & has_y[0])
    keep = keep & ((row_g >= 3) | has_x[0]) & ((row_g < 9) | has_x[1])

    for t in range(STEPS):
        for f in range(2):
            if t > 0 and f == 0:
                exchange_columns(t)
                send_x(t, 1)

            def coarse_in(d):
                x_wait_copies(t, f, d)[0].wait_recv()
                if f == 0:
                    g_copy(t, d, d).wait_recv()

            each(has_x, coarse_in)
            for q in range(3):
                cols = mg.at[t] if q == 1 else xg.at[t, q // 2]
                cols = cols[fz : fz + rows_c, :]
                for c in range(3):
                    i = 3 * f + c
                    plane = cn[t, i] if q == 1 else xc[t, q // 2, i]
                    whole = jnp.concatenate([plane, halo_tile(cols, i, lane_c)], axis=1)
                    extc[q, c, TOP : TOP + cz, :] = whole[0:cz]
                    extc[q, c, TOP - 1 : TOP, :] = whole[cz : cz + 1]
                    extc[q, c, TOP + cz : TOP + cz + 1, :] = jnp.zeros((1, cy + LANES), jnp.float32)
            laplace, grad_div = stencil(extc, 1, cz, cy, 2.0, half_c, sq_c)
            for c in range(3):
                i = 3 * f + c
                before = cold[i] if t == 0 else cn[t - 1, i, 0:cz, :]
                mu = shc[...]
                new = 2.0 * cn[t, i, 0:cz, :] - before + STEP_SQUARED * (
                    mu * laplace[c] + (lac[...] + mu) * grad_div[c]
                )
                if t < STEPS - 1:
                    cn[t + 1, i, 0:cz, :] = new
                else:
                    cout[i] = new

            ghin[...] = jnp.zeros(ghin.shape, jnp.float32)
            for c in range(3):
                low, mid, high = (extc[q, c, TOP : TOP + 1, :] for q in range(3))
                quads = (
                    0.75 * low + 0.25 * mid,
                    0.75 * mid + 0.25 * low,
                    0.75 * mid + 0.25 * high,
                    0.75 * high + 0.25 * mid,
                )
                for q in range(4):
                    ghin[3 * q + c : 3 * q + c + 1, : cy + LANES] = quads[q]
            ghost[...] = jnp.where(keep, dot(ghin[:, : cy + LANES], spread), 0.0)

            each(has_x, lambda d: x_wait_copies(t, f, d)[1].wait_recv())
            for q in range(4):
                cols = xg[t, q // 3, 0:fz, :] if q in (0, 3) else mg[t, 0:fz, :]
                x = (1, 0, 1, 0)[q]
                for c in range(3):
                    i = 3 * f + c
                    plane = xf[t, q // 3, i] if q in (0, 3) else fn[t, x, i]
                    whole = jnp.concatenate([plane, halo_tile(cols, 2 * i + x, lane_f)], axis=1)
                    ext[q, c, TOP : TOP + fz, :] = whole
                    ext[q, c, TOP - 1 : TOP, :] = whole[0:1]
                    ext[q, c, TOP + fz : TOP + fz + 1, :] = ghost[3 * q + c : 3 * q + c + 1, :]
            for x in range(2):
                laplace, grad_div = stencil(ext, x + 1, fz, fy, 1.0, half_inv, inv_sq)
                picks = [pl.ds(2 * y + x, fz, stride=2 * tiles) for y in range(tiles)]

                def fetch(*at):
                    return jnp.concatenate([at[0][at[1:] + (p, slice(None))] for p in picks], axis=1)

                mu = fetch(shf)
                both = fetch(laf) + mu
                for c in range(3):
                    i = 3 * f + c
                    before = fetch(fold, i) if t == 0 else fn[t - 1, x, i]
                    new = 2.0 * fn[t, x, i] - before + STEP_SQUARED * (
                        mu * laplace[c] + both * grad_div[c]
                    )
                    fn[t + 1, x, i] = new
                    if t == STEPS - 1:
                        for y in range(tiles):
                            fout[i, picks[y], :] = new[:, y * LANES : (y + 1) * LANES]
            if t < STEPS - 1:
                set_ridge(t + 1, f)
                if f == 0:
                    send_x(t + 1, 0)

        def later(i):
            return cn[t + 1, i, 0:cz, :] if t < STEPS - 1 else cout[i]

        prod = later(0) * later(3) + later(1) * later(4) + later(2) * later(5)
        cker[...] = prod if t == 0 else cker[...] + prod
        for x in range(2):
            prod = sum(fn[t + 1, x, c] * fn[t + 1, x, c + 3] for c in range(3))
            for y in range(tiles):
                piece = prod[:, y * LANES : (y + 1) * LANES]
                pick = pl.ds(2 * y + x, fz, stride=2 * tiles)
                fker[pick, :] = piece if t == 0 else fker[pick, :] + piece

    def finish_x(d):
        j_copy(d, d).wait_send()
        for t in range(STEPS):
            g_copy(t, d, d).wait_send()
            for f in range(2):
                for copy in x_wait_copies(t, f, d):
                    copy.wait_send()

    def finish_y(d):
        for t in range(STEPS):
            y_copy(t, d, d).wait_send()

    each(has_x, finish_x)
    each(has_y, finish_y)


def rows_view(a):
    lead = a.shape[:-3]
    fz, fx, fy = a.shape[-3:]
    n = len(lead)
    a = a.reshape(lead + (fz, fx, fy // LANES, LANES))
    a = a.transpose(tuple(range(n)) + (n, n + 2, n + 1, n + 3))
    return a.reshape(((6,) if lead else ()) + (fz * fx * fy // LANES, LANES))


def rows_back(a, shape):
    lead = shape[:-3]
    fz, fx, fy = shape[-3:]
    n = len(lead)
    a = a.reshape(lead + (fz, fy // LANES, fx, LANES))
    a = a.transpose(tuple(range(n)) + (n, n + 2, n + 1, n + 3))
    return a.reshape(shape)


def on_device(fold, fnow, cold, cnow, shf, laf, shc, lac, topo):
    nx, ny = lax.axis_size("gx"), lax.axis_size("gy")
    fz, fx, fy = shf.shape
    cz, cx, cy = shc.shape
    if fx != 2 or cx != 1 or cy != LANES or fy != 2 * cy:
        raise ValueError("unsupported tile")
    rows_c = cz + 8
    f32 = jnp.float32
    dma = pltpu.SemaphoreType.DMA
    nrows = fz * fx * fy // LANES
    vm = pl.BlockSpec(memory_space=pltpu.VMEM)
    fout, cout, fker, cker = pl.pallas_call(
        functools.partial(body, nx, ny, fz, cz, fy, cy),
        out_shape=(
            jax.ShapeDtypeStruct((6, nrows, LANES), f32),
            jax.ShapeDtypeStruct((6, cz, cy), f32),
            jax.ShapeDtypeStruct((nrows, LANES), f32),
            jax.ShapeDtypeStruct((cz, cy), f32),
        ),
        in_specs=[vm] * 9,
        out_specs=(vm,) * 4,
        scratch_shapes=[
            pltpu.VMEM((STEPS + 1, 2, 6, fz, fy), f32),
            pltpu.VMEM((STEPS, 6, rows_c, cy), f32),
            pltpu.VMEM((STEPS, 2, 6, fz, fy), f32),
            pltpu.VMEM((STEPS, 2, 6, rows_c, cy), f32),
            pltpu.VMEM((STEPS, 2, fz + rows_c, LANES), f32),
            pltpu.VMEM((STEPS, 2, fz + rows_c, LANES), f32),
            pltpu.VMEM((STEPS, 2, fz + rows_c, LANES), f32),
            pltpu.VMEM((STEPS, fz + rows_c, LANES), f32),
            pltpu.VMEM((8, fy), f32),
            pltpu.VMEM((2, 8, fy), f32),
            pltpu.VMEM((4, 3, fz + 16, fy + LANES), f32),
            pltpu.VMEM((3, 3, cz + 16, cy + LANES), f32),
            pltpu.VMEM((16, max(fy, cy + LANES)), f32),
            pltpu.VMEM((16, fy + LANES), f32),
            dma((STEPS, 2, 2, 2)),
            dma((STEPS, 2, 2, 2)),
            dma((STEPS, 2)),
            dma((STEPS, 2)),
            dma((STEPS, 2)),
            dma((STEPS, 2)),
            dma((2,)),
            dma((2,)),
        ],
        compiler_params=pltpu.CompilerParams(collective_id=0, has_side_effects=True),
        name="wave",
    )(
        rows_view(fold),
        rows_view(fnow),
        cold.reshape(6, cz, cy),
        cnow.reshape(6, cz, cy),
        rows_view(shf),
        rows_view(laf),
        shc.reshape(cz, cy),
        lac.reshape(cz, cy),
        topo,
    )
    return (
        rows_back(fout, fold.shape),
        cout.reshape(cold.shape),
        rows_back(fker, shf.shape),
        cker.reshape(shc.shape),
    )


def solution(mesh):
    field, coef = P(None, None, None, "gx", "gy"), P(None, "gx", "gy")
    return jax.shard_map(
        on_device,
        mesh=mesh,
        in_specs=(field,) * 4 + (coef,) * 4 + (P("gx", "gy"),),
        out_specs=(field, field, coef, coef),
        check_vma=False,
    )
```

time: 153 us -> 40.1 us (0.26)
  starting transfers between devices: 55 us -> 0 us
  other arithmetic: 44 us -> 0 us
  Pallas kernels: 0 us -> 34.8 us
  waiting for transfers between devices: 29.9 us -> 0 us
  local copies, waits for them, and re-layouts: 21.3 us -> 4.35 us
    ppermute x20 -> x0, starting transfers between devices: 55 us -> none  [the longest x10 35 us: with_halo(): lax.ppermute(tail, axis, [(i, (i + 1) % count) for i in range(ends)])]
    pallas_call x0 -> x1, Pallas kernels: none -> 34.8 us  [on_device(): pl.pallas_call(functools.partial(body, nx, ny, fz, cz, fy, cy), out_shape...]
    ppermute x20 -> x0, waiting for transfers between devices: 29.9 us -> none  [the longest x10 20.5 us: with_halo(): lax.ppermute(head, axis, [((i + 1) % count, i) for i in range(ends)])]
    concatenate x16 -> x0, other arithmetic: 19.5 us -> none  [the longest x12 18.8 us: with_halo(): jnp.concatenate([lax.ppermute(tail, axis, [(i, (i + 1) % count) for i in...]
    add x17 -> x0, other arithmetic: 10.4 us -> none  [the longest x4 2.81 us: accelerate(): curve_xx[:, 0] + mixed_xy[:, 1] + mixed_xz[:, 2]]
    mul x5 -> x0, other arithmetic: 9.3 us -> none  [the longest x4 9.22 us: accelerate(): (offset(padded, 0, 1, 1) - offset(padded, 0, 1, -1) - offset(padded, 0, -...]
    slice x17 -> x0, local copies, waits for them, and re-layouts: 7.27 us -> none  [the longest x8 4.04 us: with_halo(): lax.slice_in_dim(cells, cells.shape[dim] - width, cells.shape[dim], axis=...]
    another operation x5 -> x0, local copies, waits for them, and re-layouts: 5.6 us -> none  [the longest x4 5.59 us: on_device(): ghost[:, :, None]]
  transfers between devices with their start and end apart: 20 -> 0, of which waited for: 10 -> 0; matrix products, arithmetic and copies ran while one was open for 17% -> 0% of each run, Pallas kernels for 0% -> 0%
where the time goes in v1:
time: 40.1 us; the launch traced here: 39.9 us
  Pallas kernels  34.8 us (87%)
  local copies, waits for them, and re-layouts  4.35 us (11%)
  between operations  0.65 us (2%)
    pallas_call x1, Pallas kernels, on_device(): pl.pallas_call(functools.partial(body, nx, ny, fz, cz, fy, cy), out_shape...  34.8 us
    unnamed x10, local copies, waits for them, and re-layouts  4.35 us

profile of v1, /device:TPU:10, one launch (start us, length us, event | category | flops | bytes accessed | tf_op | source)
XLA Modules:
  0.0 39.9 jit_solution(9663173620358010289)
XLA Ops:
  0.6 34.8 %wave.1 = (f32[6,160,128]{2,1,0:T(8,128)}, f32[6,80,128]{2,1,0:T(8,128)}, f32[160,128]{1,0:T(8,128)}, f32[80,128]{1,0:T(8,128)}) custom-call(f32[6,160,128]{2,1,0:T(8,128)} %bitcast.41, f32[6,160,128]{2,1,0:T(8,128)} %bitcast.42, f32[6,80,128]{2,1,0:T(8,128)} %bitcast.43, f32[6,80,128]{2,1,0:T(8,128)} %bitcast.44, f32[160,128]{1,0:T(8,128)} %bitcast.47, ...), custom_call_target="tpu_custom_call" | custom-call | tf_op jit(solution)/shard_map/wave/pallas_call | solution.py:396
  35.5 0.0 copy-start
  35.5 2.0 %copy.25 = f32[2,3,40,2,256]{4,3,2,1,0:T(2,128)} copy(f32[2,3,40,2,256]{4,3,2,1,0:T(2,128)} %bitcast.40) | data formatting | bytes 983040
  37.5 0.0 copy-done
  37.5 0.0 copy-start.1
  37.5 0.7 %copy.26 = f32[2,3,80,1,128]{4,3,2,1,0:T(1,128)} copy(f32[2,3,80,1,128]{4,3,2,1,0:T(1,128)S(1)} %bitcast.45) | data formatting | bytes 491520
  38.2 0.2 copy-done.1
  38.5 0.0 copy-start.2
  38.5 0.6 %copy.27 = f32[40,2,256]{2,1,0:T(2,128)} copy(f32[40,2,256]{2,1,0:T(2,128)S(1)} %bitcast.46) | data formatting | bytes 163840
  39.1 0.1 copy-done.2
  39.2 0.6 %copy.28 = f32[80,1,128]{2,1,0:T(1,128)} copy(f32[80,1,128]{2,1,0:T(1,128)S(1)} %bitcast.49) | data formatting | bytes 81920
Async XLA Ops:
  35.5 2.0 %copy-start = (f32[6,80,128]{2,1,0:T(8,128)S(1)}, f32[6,80,128]{2,1,0:T(8,128)}, u32[]{:S(2)}) copy-start(f32[6,80,128]{2,1,0:T(8,128)} %get-tuple-element.9) | copy-start | bytes 737284
  37.5 0.9 %copy-start.1 = (f32[160,128]{1,0:T(8,128)S(1)}, f32[160,128]{1,0:T(8,128)}, u32[]{:S(2)}) copy-start(f32[160,128]{1,0:T(8,128)} %get-tuple-element.10) | copy-start | bytes 245764
  38.5 0.8 %copy-start.2 = (f32[80,128]{1,0:T(8,128)S(1)}, f32[80,128]{1,0:T(8,128)}, u32[]{:S(2)}) copy-start(f32[80,128]{1,0:T(8,128)} %get-tuple-element.11) | copy-start | bytes 122884

commit v2 on v1

--- a/solution.py
+++ b/solution.py
@@ -12,6 +12,7 @@
 LANES = 128
 HALF = LANES // 2
 TOP = 8
+FIRST, SECOND = 16, 24
 
 
 def stencil(ext, s, depth, own, grid_step, half_inv, inv_sq):
@@ -67,6 +68,7 @@
     has_y = (gy > 0, gy < ny - 1)
     tiles = fy // LANES
     rows_c = cn.shape[2]
+    split = mg.shape[1]
 
     barrier = pltpu.get_barrier_semaphore()
     for side in range(2):
@@ -207,9 +209,15 @@
             coarse = jnp.zeros((rows_c, LANES), jnp.float32)
             at = (0, cy - 1)[d]
             for i in range(6):
-                coarse = jnp.where(lane_c == base + i, cn[t, i, :, at : at + 1], coarse)
-            pk[t, d, 0:fz, :] = fine
-            pk[t, d, fz : fz + rows_c, :] = coarse
+                column = cn[t, i, :, at : at + 1]
+                coarse = jnp.where(lane_c == base + FIRST + i, column, coarse)
+                coarse = jnp.where(lane_c == base + SECOND + i, column, coarse)
+            upper = lax.broadcasted_iota(jnp.int32, (split, LANES), 1) % HALF < SECOND
+            bottom = jnp.concatenate(
+                [coarse[split:], jnp.zeros((2 * split - rows_c, LANES), jnp.float32)], axis=0
+            )
+            top = jnp.concatenate([fine, jnp.zeros((split - fz, LANES), jnp.float32)], axis=0)
+            pk[t, d] = top + jnp.where(upper, coarse[0:split], bottom)
 
     def exchange_columns(t):
         pack(t)
@@ -228,6 +236,12 @@
             v[:, HALF + k : HALF + k + 1],
             jnp.where(lane == LANES - 1, v[:, k : k + 1], 0.0),
         )
+
+    lane_s = lax.broadcasted_iota(jnp.int32, (split, LANES), 1)
+
+    def coarse_tile(v, i):
+        first, second = halo_tile(v, FIRST + i, lane_s), halo_tile(v, SECOND + i, lane_s)
+        return jnp.concatenate([first, second[: rows_c - split]], axis=0)
 
     each(has_x, lambda d: j_copy(d, d).wait_recv())
     lane_1 = lax.broadcasted_iota(jnp.int32, (1, LANES), 1)
@@ -267,11 +281,11 @@
             each(has_x, coarse_in)
             for q in range(3):
                 cols = mg.at[t] if q == 1 else xg.at[t, q // 2]
-                cols = cols[fz : fz + rows_c, :]
+                cols = cols[...]
                 for c in range(3):
                     i = 3 * f + c
                     plane = cn[t, i] if q == 1 else xc[t, q // 2, i]
-                    whole = jnp.concatenate([plane, halo_tile(cols, i, lane_c)], axis=1)
+                    whole = jnp.concatenate([plane, coarse_tile(cols, i)], axis=1)
                     extc[q, c, TOP : TOP + cz, :] = whole[0:cz]
                     extc[q, c, TOP - 1 : TOP, :] = whole[cz : cz + 1]
                     extc[q, c, TOP + cz : TOP + cz + 1, :] = jnp.zeros((1, cy + LANES), jnp.float32)
@@ -389,6 +403,7 @@
     if fx != 2 or cx != 1 or cy != LANES or fy != 2 * cy:
         raise ValueError("unsupported tile")
     rows_c = cz + 8
+    split = 8 * max(pl.cdiv(fz, 8), pl.cdiv(rows_c, 16))
     f32 = jnp.float32
     dma = pltpu.SemaphoreType.DMA
     nrows = fz * fx * fy // LANES
@@ -408,10 +423,10 @@
             pltpu.VMEM((STEPS, 6, rows_c, cy), f32),
             pltpu.VMEM((STEPS, 2, 6, fz, fy), f32),
             pltpu.VMEM((STEPS, 2, 6, rows_c, cy), f32),
-            pltpu.VMEM((STEPS, 2, fz + rows_c, LANES), f32),
-            pltpu.VMEM((STEPS, 2, fz + rows_c, LANES), f32),
-            pltpu.VMEM((STEPS, 2, fz + rows_c, LANES), f32),
-            pltpu.VMEM((STEPS, fz + rows_c, LANES), f32),
+            pltpu.VMEM((STEPS, 2, split, LANES), f32),
+            pltpu.VMEM((STEPS, 2, split, LANES), f32),
+            pltpu.VMEM((STEPS, 2, split, LANES), f32),
+            pltpu.VMEM((STEPS, split, LANES), f32),
             pltpu.VMEM((8, fy), f32),
             pltpu.VMEM((2, 8, fy), f32),
             pltpu.VMEM((4, 3, fz + 16, fy + LANES), f32),

time: 40.1 us -> 40.9 us (1.020)
  the two profiles are of different devices: /device:TPU:10 before, /device:TPU:1 now
where the time goes in v2:
time: 40.9 us; the launch traced here: 40.6 us
  Pallas kernels  35.6 us (87%)
  local copies, waits for them, and re-layouts  4.35 us (11%)
  between operations  0.65 us (2%)
    pallas_call x1, Pallas kernels, on_device(): pl.pallas_call(functools.partial(body, nx, ny, fz, cz, fy, cy), out_shape...  35.6 us
    unnamed x10, local copies, waits for them, and re-layouts  4.35 us

profile of v2, /device:TPU:1, one launch (start us, length us, event | category | flops | bytes accessed | tf_op | source)
XLA Modules:
  0.0 40.6 jit_solution(3547021362297881809)
XLA Ops:
  0.6 35.6 %wave.1 = (f32[6,160,128]{2,1,0:T(8,128)}, f32[6,80,128]{2,1,0:T(8,128)}, f32[160,128]{1,0:T(8,128)}, f32[80,128]{1,0:T(8,128)}) custom-call(f32[6,160,128]{2,1,0:T(8,128)} %bitcast.41, f32[6,160,128]{2,1,0:T(8,128)} %bitcast.42, f32[6,80,128]{2,1,0:T(8,128)} %bitcast.43, f32[6,80,128]{2,1,0:T(8,128)} %bitcast.44, f32[160,128]{1,0:T(8,128)} %bitcast.47, ...), custom_call_target="tpu_custom_call" | custom-call | tf_op jit(solution)/shard_map/wave/pallas_call | solution.py:411
  36.2 0.0 copy-start
  36.3 2.0 %copy.25 = f32[2,3,40,2,256]{4,3,2,1,0:T(2,128)} copy(f32[2,3,40,2,256]{4,3,2,1,0:T(2,128)} %bitcast.40) | data formatting | bytes 983040
  38.3 0.0 copy-done
  38.3 0.0 copy-start.1
  38.3 0.7 %copy.26 = f32[2,3,80,1,128]{4,3,2,1,0:T(1,128)} copy(f32[2,3,80,1,128]{4,3,2,1,0:T(1,128)S(1)} %bitcast.45) | data formatting | bytes 491520
  39.0 0.2 copy-done.1
  39.2 0.0 copy-start.2
  39.2 0.6 %copy.27 = f32[40,2,256]{2,1,0:T(2,128)} copy(f32[40,2,256]{2,1,0:T(2,128)S(1)} %bitcast.46) | data formatting | bytes 163840
  39.9 0.1 copy-done.2
  40.0 0.6 %copy.28 = f32[80,1,128]{2,1,0:T(1,128)} copy(f32[80,1,128]{2,1,0:T(1,128)S(1)} %bitcast.49) | data formatting | bytes 81920
Async XLA Ops:
  36.2 2.0 %copy-start = (f32[6,80,128]{2,1,0:T(8,128)S(1)}, f32[6,80,128]{2,1,0:T(8,128)}, u32[]{:S(2)}) copy-start(f32[6,80,128]{2,1,0:T(8,128)} %get-tuple-element.9) | copy-start | bytes 737284
  38.3 0.9 %copy-start.1 = (f32[160,128]{1,0:T(8,128)S(1)}, f32[160,128]{1,0:T(8,128)}, u32[]{:S(2)}) copy-start(f32[160,128]{1,0:T(8,128)} %get-tuple-element.10) | copy-start | bytes 245764
  39.2 0.8 %copy-start.2 = (f32[80,128]{1,0:T(8,128)S(1)}, f32[80,128]{1,0:T(8,128)}, u32[]{:S(2)}) copy-start(f32[80,128]{1,0:T(8,128)} %get-tuple-element.11) | copy-start | bytes 122884
